TPU v7x, 128 devices: a whole 4x4x4 slice. The times are simulated.
128 devices in a mesh: aux: 4 (over y), tile: 32 (over x, z, core).
Axes of the slice: x: 4, y: 4, z: 4, core: 2. Of those that a mesh axis runs over, the one named last changes fastest.
Arguments:
- integrals: bfloat16 [11904, 8, 2944], P(('aux', 'tile')), may hold values from -0.57421875 to 0.57421875
- coefficients: bfloat16 [2944, 2048], replicated, may hold values from -0.109375 to 0.109375
- owned_tiles: int32 [2, 64], replicated, may hold values from 0 to 63, each once within a row
- pair_list: int32 [2, 64, 4], P(None, 'tile'), may hold values from -1 to 63, as said below
- amplitudes: bfloat16 [2, 64, 4, 128, 128], P(None, 'tile'), may hold values from -0.25 to 0.25
Outputs:
- residual: float32 [2, 64, 128, 128], P(None, 'tile')
Inputs may be any that keep to these rules, and one draw needn't show every extreme that they name: `pair_list`: every live entry of slot s is a slot within 2 of s; the live entries of one slot are distinct; -1 marks an entry dropped by screening.
All inputs are finite; a program needn't handle non-finite values.
Results may differ from a plain program's by a relative error of at most 0.00087.
Values may be sent and summed in bfloat16 or wider, within the bound.
A program may use at most 128 MiB of HBM per device.

v0:
```python
import jax
import jax.numpy as jnp
from jax import lax
from jax.sharding import PartitionSpec as P

NB = 2


def per_device(integrals, coefficients, owned_tiles, pair_list, amplitudes):
    tile_count = lax.axis_size("tile")
    q_rows, occ_all, ao_count = integrals.shape
    virt_count = coefficients.shape[1]
    tile_width = amplitudes.shape[-1]
    virt_tiles = virt_count // tile_width
    per_dev = pair_list.shape[1]
    occ_batch = occ_all // NB
    total_slots = owned_tiles.shape[1]
    first_slot = lax.axis_index("tile") * per_dev
    positions = jnp.arange(3 * per_dev, dtype=jnp.int32)
    results = []
    for occ_group in range(NB):
        int_block = integrals[:, occ_group * occ_batch : (occ_group + 1) * occ_batch, :].reshape(
            q_rows * occ_batch, ao_count
        )
        half_done = jnp.dot(int_block, coefficients, preferred_element_type=jnp.float32).astype(
            jnp.bfloat16
        )
        half_done = half_done.reshape(q_rows, occ_batch * virt_tiles, tile_width)
        ordered = jnp.take(half_done, owned_tiles[occ_group], axis=1)
        zero_pad = jnp.zeros((q_rows, per_dev, tile_width), jnp.bfloat16)
        padded = jnp.concatenate([zero_pad, ordered, zero_pad], axis=1)
        below_part = padded[:, :total_slots].reshape(q_rows, tile_count, per_dev, tile_width)
        middle = ordered.reshape(q_rows, tile_count, per_dev, tile_width)
        above_part = padded[:, 2 * per_dev :].reshape(q_rows, tile_count, per_dev, tile_width)
        bundle = jnp.concatenate([below_part, middle, above_part], axis=2)
        arrived = lax.all_to_all(bundle, "tile", split_axis=1, concat_axis=0, tiled=True)
        extended = arrived.reshape(q_rows * tile_count, 3 * per_dev, tile_width)
        mine = extended[:, per_dev : 2 * per_dev]
        listed = pair_list[occ_group]
        ext_place = listed - (first_slot - per_dev)
        selector = (
            (ext_place[:, :, None] == positions[None, None, :]) & (listed[:, :, None] >= 0)
        ).astype(jnp.float32)
        amp_tiles = amplitudes[occ_group]
        cross_ints = jnp.einsum("qja,qeb->jeab", mine, extended, preferred_element_type=jnp.float32)
        partial_value = jnp.einsum(
            "jke,jeab->jkab", selector, cross_ints, precision=lax.Precision.HIGHEST
        )
        summed = lax.psum(partial_value, "aux")
        residue = jnp.einsum(
            "jkab,jkbc->jac", summed, amp_tiles.astype(jnp.float32), precision=lax.Precision.HIGHEST
        )
        results.append(residue)
    return jnp.stack(results)


def solution(mesh):
    in_specs = (
        P(("aux", "tile"), None, None),
        P(),
        P(),
        P(None, "tile", None),
        P(None, "tile", None, None, None),
    )
    out_specs = P(None, "tile", None, None)
    return jax.shard_map(
        per_device, mesh=mesh, in_specs=in_specs, out_specs=out_specs, check_vma=False
    )
```

profile of v0, /device:TPU:0, one launch (start us, length us, event | category | flops | bytes accessed | tf_op | source)
XLA Modules:
  0.0 286.1 jit_solution(10070424365951236372)
XLA Ops:
  6.5 0.8 compare_and_fusion.1
  7.3 6.6 %fusion.28 = (bf16[93,4,2944]{2,1,0:T(4,128)(2,1)}, bf16[93,4,2944]{2,1,0:T(4,128)(2,1)S(1)}) fusion(bf16[93,8,2944]{2,1,0:T(8,128)(2,1)} %param.7), kind=kLoop, calls=%fused_computation.51 | loop fusion | bytes 8761344 | tf_op jit(solution)/shard_map/slice | solution.py:22
  13.9 4.4 %reshape.75 = bf16[372,2944]{1,0:T(8,128)(2,1)} reshape(bf16[93,4,2944]{2,1,0:T(4,128)(2,1)} %get-tuple-element.12) | data formatting | bytes 4380672 | tf_op jit(solution)/shard_map/reshape | solution.py:22
  18.3 11.2 %convolution_convert_fusion.1 = bf16[372,2048]{1,0:T(8,128)(2,1)} fusion(bf16[372,2944]{1,0:T(8,128)(2,1)} %reshape.75, bf16[2944,2048]{1,0:T(8,128)(2,1)} %param.8), kind=kOutput, calls=%fused_computation.9 | convolution fusion | flops 4486569984 | bytes 15772672 | tf_op jit(solution)/shard_map/dot_general | solution.py:25
  29.5 3.7 %reshape.76 = bf16[93,64,128]{2,1,0:T(8,128)(2,1)} reshape(bf16[372,2048]{1,0:T(8,128)(2,1)} %convolution_convert_fusion.1) | data formatting | bytes 3047424 | tf_op jit(solution)/shard_map/reshape | solution.py:28
  33.2 3.6 %copy.14 = bf16[93,64,128]{2,0,1:T(8,128)(2,1)} copy(bf16[93,64,128]{2,1,0:T(8,128)(2,1)} %reshape.76) | data formatting | bytes 3047424 | tf_op jit(solution)/shard_map/reshape | solution.py:28
  36.8 2.6 reshape.81
  39.4 10.0 %convolution_convert_fusion = bf16[372,2048]{1,0:T(8,128)(2,1)S(1)} fusion(bf16[372,2944]{1,0:T(8,128)(2,1)} %reshape.81, bf16[2944,2048]{1,0:T(8,128)(2,1)} %param.8), kind=kOutput, calls=%fused_computation.8 | convolution fusion | flops 4486569984 | bytes 15772672 | tf_op jit(solution)/shard_map/dot_general | solution.py:25
  49.4 1.8 reshape.82
  51.3 2.5 copy.18
  53.8 1.9 gather_fusion
  55.7 1.9 gather_fusion.1
  57.6 2.2 broadcast_select_fusion
  60.3 2.5 pad_maximum_fusion
  62.7 8.4 %all-to-all-start = ((bf16[93,32,6,128]{3,0,2,1:T(8,128)(2,1)}), bf16[93,32,6,128]{3,0,2,1:T(8,128)(2,1)}, u32[]{:S(2)}, u32[]{:S(2)}) async-start(bf16[93,32,6,128]{3,0,2,1:T(8,128)(2,1)} %pad_maximum_fusion), calls=%async_computation | async-start | bytes 9437184 | tf_op jit(solution)/shard_map/all_to_all | solution.py:36
  71.5 2.4 pad_maximum_fusion.1
  73.9 56.1 %all-to-all-done = bf16[93,32,6,128]{3,0,2,1:T(8,128)(2,1)} async-done(((bf16[93,32,6,128]{3,0,2,1:T(8,128)(2,1)}), bf16[93,32,6,128]{3,0,2,1:T(8,128)(2,1)}, u32[]{:S(2)}, u32[]{:S(2)}) %all-to-all-start) | async-done | bytes 4571168 | tf_op jit(solution)/shard_map/all_to_all | solution.py:36
  130.0 7.2 %all-to-all-start.1 = ((bf16[93,32,6,128]{3,0,2,1:T(8,128)(2,1)}), bf16[93,32,6,128]{3,0,2,1:T(8,128)(2,1)}, u32[]{:S(2)}, u32[]{:S(2)}) async-start(bf16[93,32,6,128]{3,0,2,1:T(8,128)(2,1)} %pad_maximum_fusion.1), calls=%async_computation.1 | async-start | bytes 9437184 | tf_op jit(solution)/shard_map/all_to_all | solution.py:36
  137.4 5.5 %copy.15 = bf16[32,93,1,6,128]{4,1,0,3,2:T(8,128)(2,1)} copy(bf16[32,93,1,6,128]{4,1,3,0,2:T(8,128)(2,1)} %bitcast.10) | data formatting | bytes 9142272 | tf_op jit(solution)/shard_map/all_to_all | solution.py:36
  142.9 7.4 %reshape.109 = bf16[2976,6,128,1]{2,0,1,3:T(8,128)(2,1)} reshape(bf16[32,93,1,6,128]{4,1,0,3,2:T(8,128)(2,1)} %copy.15) | data formatting | bytes 9142272 | tf_op jit(solution)/shard_map/reshape | solution.py:37
  150.3 7.3 %reshape.80 = bf16[2976,6,128]{2,0,1:T(8,128)(2,1)} reshape(bf16[32,93,1,6,128]{4,1,0,3,2:T(8,128)(2,1)} %copy.15) | data formatting | bytes 9142272 | tf_op jit(solution)/shard_map/reshape | solution.py:37
  157.6 38.8 %all-to-all-done.1 = bf16[93,32,6,128]{3,0,2,1:T(8,128)(2,1)} async-done(((bf16[93,32,6,128]{3,0,2,1:T(8,128)(2,1)}), bf16[93,32,6,128]{3,0,2,1:T(8,128)(2,1)}, u32[]{:S(2)}, u32[]{:S(2)}) %all-to-all-start.1) | async-done | bytes 4571168 | tf_op jit(solution)/shard_map/all_to_all | solution.py:36
  196.4 5.5 %copy.19 = bf16[32,93,1,6,128]{4,1,0,3,2:T(8,128)(2,1)} copy(bf16[32,93,1,6,128]{4,1,3,0,2:T(8,128)(2,1)} %bitcast.28) | data formatting | bytes 9142272 | tf_op jit(solution)/shard_map/all_to_all | solution.py:36
  201.9 7.4 %reshape.113 = bf16[2976,6,128,1]{2,0,1,3:T(8,128)(2,1)} reshape(bf16[32,93,1,6,128]{4,1,0,3,2:T(8,128)(2,1)} %copy.19) | data formatting | bytes 9142272 | tf_op jit(solution)/shard_map/reshape | solution.py:37
  209.3 7.4 %reshape.86 = bf16[2976,6,128]{2,0,1:T(8,128)(2,1)} reshape(bf16[32,93,1,6,128]{4,1,0,3,2:T(8,128)(2,1)} %copy.19) | data formatting | bytes 9142272 | tf_op jit(solution)/shard_map/reshape | solution.py:37
  216.6 4.2 %fusion.4 = f32[2,6,128,128]{2,3,0,1:T(8,128)S(1)} fusion(bf16[2976,6,128]{2,0,1:T(8,128)(2,1)} %reshape.80, bf16[2976,6,128,1]{2,0,1,3:T(8,128)(2,1)} %reshape.109), kind=kOutput, calls=%fused_computation.18 | convolution fusion | flops 1170210816 | bytes 6881280 | tf_op jit(solution)/shard_map/qja,qeb->jeab/dot_general | solution.py:45
  221.3 4.2 %fusion.7 = f32[2,6,128,128]{2,3,0,1:T(8,128)S(1)} fusion(bf16[2976,6,128]{2,0,1:T(8,128)(2,1)} %reshape.86, bf16[2976,6,128,1]{2,0,1,3:T(8,128)(2,1)} %reshape.113), kind=kOutput, calls=%fused_computation.19 | convolution fusion | flops 1170210816 | bytes 6881280 | tf_op jit(solution)/shard_map/qja,qeb->jeab/dot_general | solution.py:45
  225.9 1.5 fusion.18
  227.3 1.5 fusion.22
  228.8 46.9 %all-reduce.7.cloned.1.call-done = (f32[2,4,128,128]{3,1,2,0:T(4,128)}, f32[2,4,128,128]{3,1,2,0:T(4,128)}) async-done(((f32[2,4,128,128]{3,1,2,0:T(4,128)}, f32[2,4,128,128]{3,1,2,0:T(4,128)}), (f32[2,4,128,128]{3,1,2,0:T(4,128)}, f32[2,4,128,128]{3,1,2,0:T(4,128)})) %all-reduce.7.cloned.1.call-update) | async-done | bytes 1048592 | tf_op jit(solution)/shard_map/psum | solution.py:49
  275.7 1.4 convolution_bitcast_fusion
  277.1 1.4 convolution_bitcast_fusion.1
  (17 shorter events, 2.5 us)
Async XLA Ops:
  51.3 2.5 copy-start
  62.7 67.3 %all-to-all-start = ((bf16[93,32,6,128]{3,0,2,1:T(8,128)(2,1)}), bf16[93,32,6,128]{3,0,2,1:T(8,128)(2,1)}, u32[]{:S(2)}, u32[]{:S(2)}) async-start(bf16[93,32,6,128]{3,0,2,1:T(8,128)(2,1)} %pad_maximum_fusion), calls=%async_computation | async-start | bytes 9437184 | tf_op jit(solution)/shard_map/all_to_all | solution.py:36
  73.9 63.4 %copy-start.2 = (s32[2,2,4]{2,1,0:T(2,128)S(1)}, s32[2,2,4]{2,1,0:T(2,128)}, u32[]{:S(2)}) copy-start(s32[2,2,4]{2,1,0:T(2,128)} %param.10) | copy-start | bytes 196
  130.0 66.4 %all-to-all-start.1 = ((bf16[93,32,6,128]{3,0,2,1:T(8,128)(2,1)}), bf16[93,32,6,128]{3,0,2,1:T(8,128)(2,1)}, u32[]{:S(2)}, u32[]{:S(2)}) async-start(bf16[93,32,6,128]{3,0,2,1:T(8,128)(2,1)} %pad_maximum_fusion.1), calls=%async_computation.1 | async-start | bytes 9437184 | tf_op jit(solution)/shard_map/all_to_all | solution.py:36
  137.3 138.4 %all-reduce.7.cloned.1.call-start = ((), (), s32[]{:S(2)}) async-start(), calls=%async_computation.2 | async-start | bytes 2097152 | tf_op jit(solution)/shard_map/psum | solution.py:49
  225.9 49.8 %copy-start.1 = (bf16[2,2,4,128,128]{4,3,2,1,0:T(8,128)(2,1)S(1)}, bf16[2,2,4,128,128]{4,3,2,1,0:T(8,128)(2,1)}, u32[]{:S(2)}) copy-start(bf16[2,2,4,128,128]{4,3,2,1,0:T(8,128)(2,1)} %param.11) | copy-start | bytes 1572868
Sparse Core Ops, SparseCore 0:
  228.9 46.7 all-reduce.6
where the time goes:
time: 287 us; the launch traced here: 286 us
  waiting for transfers between devices  142 us (49%)
  local copies, waits for them, and re-layouts  71.2 us (25%)
  matrix products  35.3 us (12%)
  starting transfers between devices  15.6 us (5%)
  between operations  13.5 us (5%)
  other arithmetic  8.62 us (3%)
    all_to_all x2, waiting for transfers between devices, per_device(): lax.all_to_all(bundle, 'tile', split_axis=1, concat_axis=0, tiled=True)  94.9 us
    psum x1, waiting for transfers between devices, per_device(): summed = lax.psum(partial_value, 'aux')  46.9 us
    reshape x4, local copies, waits for them, and re-layouts, per_device(): extended = arrived.reshape(q_rows * tile_count, 3 * per_dev, tile_width)  29.5 us
    dot_general x2, matrix products, per_device(): jnp.dot(int_block, coefficients, preferred_element_type=jnp.float32)  21.2 us
    all_to_all x2, starting transfers between devices, per_device(): lax.all_to_all(bundle, 'tile', split_axis=1, concat_axis=0, tiled=True)  15.6 us
    reshape x4, local copies, waits for them, and re-layouts, per_device(): half_done = half_done.reshape(q_rows, occ_batch * virt_tiles, tile_width)  11.6 us
    all_to_all x2, local copies, waits for them, and re-layouts, per_device(): lax.all_to_all(bundle, 'tile', split_axis=1, concat_axis=0, tiled=True)  11 us
    dot_general x2, matrix products, per_device(): jnp.einsum('qja,qeb->jeab', mine, extended, preferred_element_type=jnp.fl...  8.4 us
  transfers between devices with their start and end apart: 3, of which 3 were waited for; matrix products, arithmetic and copies ran while one was open for 8% of the time, Pallas kernels for 0%

commit v1 on v0

--- a/solution.py
+++ b/solution.py
@@ -46,7 +46,9 @@
         partial_value = jnp.einsum(
             "jke,jeab->jkab", selector, cross_ints, precision=lax.Precision.HIGHEST
         )
-        summed = lax.psum(partial_value, "aux")
+        summed = partial_value
+        for hop in (1, 2):
+            summed = summed + lax.ppermute(summed, "aux", [(dev, dev ^ hop) for dev in range(4)])
         residue = jnp.einsum(
             "jkab,jkbc->jac", summed, amp_tiles.astype(jnp.float32), precision=lax.Precision.HIGHEST
         )

time: 287 us -> 269 us (0.937)
  between operations: 13.5 us -> 0.19 us
  waiting for transfers between devices: 142 us -> 129 us
  starting transfers between devices: 15.6 us -> 24.6 us
  matrix products: 35.3 us -> 31.6 us
    psum x1 -> x0, waiting for transfers between devices: 46.9 us -> none  [per_device(): summed = lax.psum(partial_value, 'aux')]
    ppermute x0 -> x4, waiting for transfers between devices: none -> 34.9 us  [per_device(): lax.ppermute(summed, 'aux', [(dev, dev ^ hop) for dev in range(4)])]
    ppermute x0 -> x4, starting transfers between devices: none -> 8.73 us  [per_device(): lax.ppermute(summed, 'aux', [(dev, dev ^ hop) for dev in range(4)])]
  transfers between devices with their start and end apart: 3 -> 6, of which waited for: 3 -> 6; matrix products, arithmetic and copies ran while one was open for 8% -> 11% of each run, Pallas kernels for 0% -> 0%
where the time goes in v1:
time: 269 us; the launch traced here: 266 us
  waiting for transfers between devices  129 us (48%)
  local copies, waits for them, and re-layouts  71.1 us (26%)
  matrix products  31.6 us (12%)
  starting transfers between devices  24.6 us (9%)
  other arithmetic  9.15 us (3%)
    all_to_all x2, waiting for transfers between devices, per_device(): lax.all_to_all(bundle, 'tile', split_axis=1, concat_axis=0, tiled=True)  94.6 us
    ppermute x4, waiting for transfers between devices, per_device(): lax.ppermute(summed, 'aux', [(dev, dev ^ hop) for dev in range(4)])  34.9 us
    reshape x4, local copies, waits for them, and re-layouts, per_device(): extended = arrived.reshape(q_rows * tile_count, 3 * per_dev, tile_width)  29.5 us
    dot_general x2, matrix products, per_device(): jnp.dot(int_block, coefficients, preferred_element_type=jnp.float32)  21.2 us
    all_to_all x2, starting transfers between devices, per_device(): lax.all_to_all(bundle, 'tile', split_axis=1, concat_axis=0, tiled=True)  15.8 us
    reshape x4, local copies, waits for them, and re-layouts, per_device(): half_done = half_done.reshape(q_rows, occ_batch * virt_tiles, tile_width)  11.6 us
    all_to_all x2, local copies, waits for them, and re-layouts, per_device(): lax.all_to_all(bundle, 'tile', split_axis=1, concat_axis=0, tiled=True)  11 us
    ppermute x4, starting transfers between devices, per_device(): lax.ppermute(summed, 'aux', [(dev, dev ^ hop) for dev in range(4)])  8.73 us
  transfers between devices with their start and end apart: 6, of which 6 were waited for; matrix products, arithmetic and copies ran while one was open for 11% of the time, Pallas kernels for 0%

profile of v1, /device:TPU:0, one launch (start us, length us, event | category | flops | bytes accessed | tf_op | source)
XLA Modules:
  0.0 266.1 jit_solution(13592112630763782113)
XLA Ops:
  0.8 6.6 %fusion.28 = (bf16[93,4,2944]{2,1,0:T(4,128)(2,1)}, bf16[93,4,2944]{2,1,0:T(4,128)(2,1)S(1)}) fusion(bf16[93,8,2944]{2,1,0:T(8,128)(2,1)} %param.7), kind=kLoop, calls=%fused_computation.51 | loop fusion | bytes 8761344 | tf_op jit(solution)/shard_map/slice | solution.py:22
  7.4 4.4 %reshape.75 = bf16[372,2944]{1,0:T(8,128)(2,1)} reshape(bf16[93,4,2944]{2,1,0:T(4,128)(2,1)} %get-tuple-element.10) | data formatting | bytes 4380672 | tf_op jit(solution)/shard_map/reshape | solution.py:22
  11.8 11.2 %convolution_convert_fusion.1 = bf16[372,2048]{1,0:T(8,128)(2,1)} fusion(bf16[372,2944]{1,0:T(8,128)(2,1)} %reshape.75, bf16[2944,2048]{1,0:T(8,128)(2,1)} %param.8), kind=kOutput, calls=%fused_computation.9 | convolution fusion | flops 4486569984 | bytes 15772672 | tf_op jit(solution)/shard_map/dot_general | solution.py:25
  22.9 3.7 %reshape.76 = bf16[93,64,128]{2,1,0:T(8,128)(2,1)} reshape(bf16[372,2048]{1,0:T(8,128)(2,1)} %convolution_convert_fusion.1) | data formatting | bytes 3047424 | tf_op jit(solution)/shard_map/reshape | solution.py:28
  26.6 3.5 %copy.18 = bf16[93,64,128]{2,0,1:T(8,128)(2,1)} copy(bf16[93,64,128]{2,1,0:T(8,128)(2,1)} %reshape.76) | data formatting | bytes 3047424 | tf_op jit(solution)/shard_map/reshape | solution.py:28
  30.2 2.6 reshape.81
  32.8 10.0 %convolution_convert_fusion = bf16[372,2048]{1,0:T(8,128)(2,1)S(1)} fusion(bf16[372,2944]{1,0:T(8,128)(2,1)} %reshape.81, bf16[2944,2048]{1,0:T(8,128)(2,1)} %param.8), kind=kOutput, calls=%fused_computation.8 | convolution fusion | flops 4486569984 | bytes 15772672 | tf_op jit(solution)/shard_map/dot_general | solution.py:25
  42.9 1.8 reshape.82
  44.7 2.5 copy.22
  47.2 1.9 gather_fusion
  49.1 1.9 gather_fusion.1
  51.0 2.2 broadcast_select_fusion
  53.7 2.5 pad_maximum_fusion
  56.1 8.4 %all-to-all-start = ((bf16[93,32,6,128]{3,0,2,1:T(8,128)(2,1)}), bf16[93,32,6,128]{3,0,2,1:T(8,128)(2,1)}, u32[]{:S(2)}, u32[]{:S(2)}) async-start(bf16[93,32,6,128]{3,0,2,1:T(8,128)(2,1)} %pad_maximum_fusion), calls=%async_computation | async-start | bytes 9437184 | tf_op jit(solution)/shard_map/all_to_all | solution.py:36
  64.9 2.4 pad_maximum_fusion.1
  67.4 56.1 %all-to-all-done = bf16[93,32,6,128]{3,0,2,1:T(8,128)(2,1)} async-done(((bf16[93,32,6,128]{3,0,2,1:T(8,128)(2,1)}), bf16[93,32,6,128]{3,0,2,1:T(8,128)(2,1)}, u32[]{:S(2)}, u32[]{:S(2)}) %all-to-all-start) | async-done | bytes 4571168 | tf_op jit(solution)/shard_map/all_to_all | solution.py:36
  123.5 7.5 %all-to-all-start.1 = ((bf16[93,32,6,128]{3,0,2,1:T(8,128)(2,1)}), bf16[93,32,6,128]{3,0,2,1:T(8,128)(2,1)}, u32[]{:S(2)}, u32[]{:S(2)}) async-start(bf16[93,32,6,128]{3,0,2,1:T(8,128)(2,1)} %pad_maximum_fusion.1), calls=%async_computation.1 | async-start | bytes 9437184 | tf_op jit(solution)/shard_map/all_to_all | solution.py:36
  131.0 5.5 %copy.19 = bf16[32,93,1,6,128]{4,1,0,3,2:T(8,128)(2,1)} copy(bf16[32,93,1,6,128]{4,1,3,0,2:T(8,128)(2,1)} %bitcast.10) | data formatting | bytes 9142272 | tf_op jit(solution)/shard_map/all_to_all | solution.py:36
  136.5 7.4 %reshape.109 = bf16[2976,6,128,1]{2,0,1,3:T(8,128)(2,1)} reshape(bf16[32,93,1,6,128]{4,1,0,3,2:T(8,128)(2,1)} %copy.19) | data formatting | bytes 9142272 | tf_op jit(solution)/shard_map/reshape | solution.py:37
  143.9 7.4 %reshape.80 = bf16[2976,6,128]{2,0,1:T(8,128)(2,1)} reshape(bf16[32,93,1,6,128]{4,1,0,3,2:T(8,128)(2,1)} %copy.19) | data formatting | bytes 9142272 | tf_op jit(solution)/shard_map/reshape | solution.py:37
  151.2 38.5 %all-to-all-done.1 = bf16[93,32,6,128]{3,0,2,1:T(8,128)(2,1)} async-done(((bf16[93,32,6,128]{3,0,2,1:T(8,128)(2,1)}), bf16[93,32,6,128]{3,0,2,1:T(8,128)(2,1)}, u32[]{:S(2)}, u32[]{:S(2)}) %all-to-all-start.1) | async-done | bytes 4571168 | tf_op jit(solution)/shard_map/all_to_all | solution.py:36
  189.7 5.5 %copy.23 = bf16[32,93,1,6,128]{4,1,0,3,2:T(8,128)(2,1)} copy(bf16[32,93,1,6,128]{4,1,3,0,2:T(8,128)(2,1)} %bitcast.28) | data formatting | bytes 9142272 | tf_op jit(solution)/shard_map/all_to_all | solution.py:36
  195.2 7.4 %reshape.113 = bf16[2976,6,128,1]{2,0,1,3:T(8,128)(2,1)} reshape(bf16[32,93,1,6,128]{4,1,0,3,2:T(8,128)(2,1)} %copy.23) | data formatting | bytes 9142272 | tf_op jit(solution)/shard_map/reshape | solution.py:37
  202.5 7.3 %reshape.86 = bf16[2976,6,128]{2,0,1:T(8,128)(2,1)} reshape(bf16[32,93,1,6,128]{4,1,0,3,2:T(8,128)(2,1)} %copy.23) | data formatting | bytes 9142272 | tf_op jit(solution)/shard_map/reshape | solution.py:37
  209.9 4.2 %fusion.4 = f32[2,6,128,128]{2,3,0,1:T(8,128)S(1)} fusion(bf16[2976,6,128]{2,0,1:T(8,128)(2,1)} %reshape.80, bf16[2976,6,128,1]{2,0,1,3:T(8,128)(2,1)} %reshape.109), kind=kOutput, calls=%fused_computation.18 | convolution fusion | flops 1170210816 | bytes 6881280 | tf_op jit(solution)/shard_map/qja,qeb->jeab/dot_general | solution.py:45
  216.8 4.2 %fusion.7 = f32[2,6,128,128]{2,3,0,1:T(8,128)S(1)} fusion(bf16[2976,6,128]{2,0,1:T(8,128)(2,1)} %reshape.86, bf16[2976,6,128,1]{2,0,1,3:T(8,128)(2,1)} %reshape.113), kind=kOutput, calls=%fused_computation.19 | convolution fusion | flops 1170210816 | bytes 6881280 | tf_op jit(solution)/shard_map/qja,qeb->jeab/dot_general | solution.py:45
  222.6 7.5 %collective-permute-done = f32[2,4,128,128]{3,1,2,0:T(4,128)S(1)} collective-permute-done((f32[2,4,128,128]{3,1,2,0:T(4,128)S(1)}, f32[2,4,128,128]{3,1,2,0:T(4,128)S(1)}, u32[]{:S(2)}, u32[]{:S(2)}) %collective-permute-start) | collective-permute-done | bytes 524320 | tf_op jit(solution)/shard_map/ppermute | solution.py:51
  230.2 3.3 %collective-permute-start.1 = (f32[2,4,128,128]{3,1,2,0:T(4,128)S(1)}, f32[2,4,128,128]{3,1,2,0:T(4,128)S(1)}, u32[]{:S(2)}, u32[]{:S(2)}) collective-permute-start(f32[2,4,128,128]{3,1,2,0:T(4,128)S(1)} %add.27), channel_id=1, source_target_pairs={{0,64},{32,96},{64,0},{96,32},{1,65},{33,97},{65,1},{97,33},{2,66}... | collective-permute-start | bytes 1572872 | tf_op jit(solution)/shard_map/ppermute | solution.py:51
  233.5 7.8 %collective-permute-done.2 = f32[2,4,128,128]{3,1,2,0:T(4,128)S(1)} collective-permute-done((f32[2,4,128,128]{3,1,2,0:T(4,128)S(1)}, f32[2,4,128,128]{3,1,2,0:T(4,128)S(1)}, u32[]{:S(2)}, u32[]{:S(2)}) %collective-permute-start.2) | collective-permute-done | bytes 524320 | tf_op jit(solution)/shard_map/ppermute | solution.py:51
  241.4 3.3 %collective-permute-start.3 = (f32[2,4,128,128]{3,1,2,0:T(4,128)S(1)}, f32[2,4,128,128]{3,1,2,0:T(4,128)S(1)}, u32[]{:S(2)}, u32[]{:S(2)}) collective-permute-start(f32[2,4,128,128]{3,1,2,0:T(4,128)S(1)} %add.29), channel_id=1, source_target_pairs={{0,64},{32,96},{64,0},{96,32},{1,65},{33,97},{65,1},{97,33},{2,66}... | collective-permute-start | bytes 1572872 | tf_op jit(solution)/shard_map/ppermute | solution.py:51
  244.7 10.3 %collective-permute-done.1 = f32[2,4,128,128]{3,1,2,0:T(4,128)S(1)} collective-permute-done((f32[2,4,128,128]{3,1,2,0:T(4,128)S(1)}, f32[2,4,128,128]{3,1,2,0:T(4,128)S(1)}, u32[]{:S(2)}, u32[]{:S(2)}) %collective-permute-start.1) | collective-permute-done | bytes 524320 | tf_op jit(solution)/shard_map/ppermute | solution.py:51
  255.5 9.3 %collective-permute-done.3 = f32[2,4,128,128]{3,1,2,0:T(4,128)S(1)} collective-permute-done((f32[2,4,128,128]{3,1,2,0:T(4,128)S(1)}, f32[2,4,128,128]{3,1,2,0:T(4,128)S(1)}, u32[]{:S(2)}, u32[]{:S(2)}) %collective-permute-start.3) | collective-permute-done | bytes 524320 | tf_op jit(solution)/shard_map/ppermute | solution.py:51
  (26 shorter events, 7.9 us)
Async XLA Ops:
  44.7 2.5 copy-start
  56.1 67.3 %all-to-all-start = ((bf16[93,32,6,128]{3,0,2,1:T(8,128)(2,1)}), bf16[93,32,6,128]{3,0,2,1:T(8,128)(2,1)}, u32[]{:S(2)}, u32[]{:S(2)}) async-start(bf16[93,32,6,128]{3,0,2,1:T(8,128)(2,1)} %pad_maximum_fusion), calls=%async_computation | async-start | bytes 9437184 | tf_op jit(solution)/shard_map/all_to_all | solution.py:36
  67.3 63.6 %copy-start.2 = (s32[2,2,4]{2,1,0:T(2,128)S(1)}, s32[2,2,4]{2,1,0:T(2,128)}, u32[]{:S(2)}) copy-start(s32[2,2,4]{2,1,0:T(2,128)} %param.10) | copy-start | bytes 196
  123.5 66.2 %all-to-all-start.1 = ((bf16[93,32,6,128]{3,0,2,1:T(8,128)(2,1)}), bf16[93,32,6,128]{3,0,2,1:T(8,128)(2,1)}, u32[]{:S(2)}, u32[]{:S(2)}) async-start(bf16[93,32,6,128]{3,0,2,1:T(8,128)(2,1)} %pad_maximum_fusion.1), calls=%async_computation.1 | async-start | bytes 9437184 | tf_op jit(solution)/shard_map/all_to_all | solution.py:36
  215.1 14.9 %collective-permute-start = (f32[2,4,128,128]{3,1,2,0:T(4,128)S(1)}, f32[2,4,128,128]{3,1,2,0:T(4,128)S(1)}, u32[]{:S(2)}, u32[]{:S(2)}) collective-permute-start(f32[2,4,128,128]{3,1,2,0:T(4,128)S(1)} %fusion.18), channel_id=1, source_target_pairs={{0,32},{32,0},{64,96},{96,64},{1,33},{33,1},{65,97},{97,65},{2,34}... | collective-permute-start | bytes 1572872 | tf_op jit(solution)/shard_map/ppermute | solution.py:51
  222.0 33.1 %copy-start.1 = (bf16[2,2,4,128,128]{4,3,2,1,0:T(8,128)(2,1)S(1)}, bf16[2,2,4,128,128]{4,3,2,1,0:T(8,128)(2,1)}, u32[]{:S(2)}) copy-start(bf16[2,2,4,128,128]{4,3,2,1,0:T(8,128)(2,1)} %param.11) | copy-start | bytes 1572868
  222.1 19.2 %collective-permute-start.2 = (f32[2,4,128,128]{3,1,2,0:T(4,128)S(1)}, f32[2,4,128,128]{3,1,2,0:T(4,128)S(1)}, u32[]{:S(2)}, u32[]{:S(2)}) collective-permute-start(f32[2,4,128,128]{3,1,2,0:T(4,128)S(1)} %fusion.22), channel_id=1, source_target_pairs={{0,32},{32,0},{64,96},{96,64},{1,33},{33,1},{65,97},{97,65},{2,34}... | collective-permute-start | bytes 1572872 | tf_op jit(solution)/shard_map/ppermute | solution.py:51
  230.2 24.8 %collective-permute-start.1 = (f32[2,4,128,128]{3,1,2,0:T(4,128)S(1)}, f32[2,4,128,128]{3,1,2,0:T(4,128)S(1)}, u32[]{:S(2)}, u32[]{:S(2)}) collective-permute-start(f32[2,4,128,128]{3,1,2,0:T(4,128)S(1)} %add.27), channel_id=1, source_target_pairs={{0,64},{32,96},{64,0},{96,32},{1,65},{33,97},{65,1},{97,33},{2,66}... | collective-permute-start | bytes 1572872 | tf_op jit(solution)/shard_map/ppermute | solution.py:51
  241.4 23.4 %collective-permute-start.3 = (f32[2,4,128,128]{3,1,2,0:T(4,128)S(1)}, f32[2,4,128,128]{3,1,2,0:T(4,128)S(1)}, u32[]{:S(2)}, u32[]{:S(2)}) collective-permute-start(f32[2,4,128,128]{3,1,2,0:T(4,128)S(1)} %add.29), channel_id=1, source_target_pairs={{0,64},{32,96},{64,0},{96,32},{1,65},{33,97},{65,1},{97,33},{2,66}... | collective-permute-start | bytes 1572872 | tf_op jit(solution)/shard_map/ppermute | solution.py:51
